TPU v7x, 256 devices: a whole 4x4x8 slice. The times are simulated.
256 devices in a mesh: band: 4 (over z_lo, core), slab: 64 (over y, x, z_hi).
Axes of the slice: x: 4, y: 4, z: 8 (z_hi: 4, z_lo: 2; z = z_hi * 2 + z_lo), core: 2. Of those that a mesh axis runs over, the one named last changes fastest.
Arguments:
- orbitals: float32 [16, 128, 128, 128], P('band', 'slab'), may hold values from -6 to 6
Outputs:
- spectrum: float32 [128, 128, 128], P('slab', None, 'band')
All inputs are finite; a program needn't handle non-finite values.
Results may differ from a plain program's by a relative error of at most 0.0043.
Values may be sent and summed in bfloat16 or wider, within the bound.
A program may use at most 64 MiB of HBM per device.

v0:
```python
import math

import jax
import jax.numpy as jnp
from jax import lax
from jax.sharding import PartitionSpec as P

SHIFTS = 2


def from_behind(value, axis, steps):
    count = lax.axis_size(axis)
    pairs = [(source, (source + steps) % count) for source in range(count)]
    return lax.ppermute(value, axis, pairs)


def dft_tables(grid_len):
    positions = jnp.arange(grid_len, dtype=jnp.int32)
    phase = positions[:, None] * positions[None, :] % grid_len
    angle = phase.astype(jnp.float32) * (2.0 * math.pi / grid_len)
    factor = 1.0 / math.sqrt(grid_len)
    cosine = jnp.cos(angle) * factor
    sine = -jnp.sin(angle) * factor
    real_table = jnp.stack([cosine, sine]).astype(jnp.bfloat16)
    complex_table = jnp.stack([jnp.stack([cosine, -sine]), jnp.stack([sine, cosine])]).astype(
        jnp.bfloat16
    )
    return (real_table, complex_table)


def form_pairs(own_rows, partner):
    return (
        (own_rows[:, None] * partner[None]).reshape((-1,) + partner.shape[1:]).astype(jnp.bfloat16)
    )


def two_passes(pairs, row_table, complex_table):
    first_pass = jnp.einsum(
        "pxyz,dkz->pdxyk", pairs, row_table, preferred_element_type=jnp.float32
    ).astype(jnp.bfloat16)
    return jnp.einsum(
        "pcxyz,dcky->pdxkz", first_pass, complex_table, preferred_element_type=jnp.float32
    ).astype(jnp.bfloat16)


def local(orbitals):
    orb_count = orbitals.shape[0]
    grid_len = orbitals.shape[2]
    slab_count = lax.axis_size("slab")
    band_count = lax.axis_size("band")
    real_table, complex_table = dft_tables(grid_len)

    def spectral_power(exchanged):
        third_pass = jnp.einsum(
            "pcxyz,dckx->pdkyz", exchanged, complex_table, preferred_element_type=jnp.float32
        )
        return jnp.sum(third_pass * third_pass, axis=1)

    local_rows = grid_len // slab_count
    accumulated = jnp.zeros((grid_len, local_rows, grid_len), jnp.float32)
    group = 1
    partner = orbitals
    for shift_step in range(SHIFTS):
        partner = from_behind(partner, "band", 1)

        def some_orbitals(position, running):
            own_rows = lax.dynamic_slice_in_dim(orbitals, position * group, group, 0)
            pairs = form_pairs(own_rows, partner)
            second_pass = two_passes(pairs, real_table, complex_table)
            power = spectral_power(
                lax.all_to_all(second_pass, "slab", split_axis=3, concat_axis=2, tiled=True)
            )
            return running + jnp.sum(power, axis=0)

        accumulated = lax.fori_loop(0, orb_count // group, some_orbitals, accumulated)
    returned = lax.all_to_all(accumulated, "slab", split_axis=0, concat_axis=1, tiled=True)
    own_share = lax.psum_scatter(returned, "band", scatter_dimension=2, tiled=True)
    pair_count = float(band_count * SHIFTS * orb_count * orb_count)
    return own_share / pair_count


def solution(mesh):
    return jax.shard_map(
        local,
        mesh=mesh,
        in_specs=(P("band", "slab", None, None),),
        out_specs=P("slab", None, "band"),
        check_vma=False,
    )
```

profile of v0, /device:TPU:1, one launch (start us, length us, event | category | flops | bytes accessed | tf_op | source)
XLA Modules:
  0.0 298.3 jit_solution(14181142731451982413)
XLA Ops:
  6.5 3.0 %collective-permute-start = (f32[4,2,128,128]{3,2,1,0:T(8,128)}, f32[4,2,128,128]{3,2,1,0:T(8,128)}, u32[]{:S(2)}, u32[]{:S(2)}) collective-permute-start(f32[4,2,128,128]{3,2,1,0:T(8,128)} %param.5), channel_id=1, source_target_pairs={{0,64},{64,128},{128,192},{192,0},{1,65},{65,129},{129,193},{193,1... | collective-permute-start | bytes 1572872 | tf_op jit(solution)/shard_map/ppermute | solution.py:14
  10.2 5.8 %collective-permute-done = f32[4,2,128,128]{3,2,1,0:T(8,128)} collective-permute-done((f32[4,2,128,128]{3,2,1,0:T(8,128)}, f32[4,2,128,128]{3,2,1,0:T(8,128)}, u32[]{:S(2)}, u32[]{:S(2)}) %collective-permute-start) | collective-permute-done | bytes 524320 | tf_op jit(solution)/shard_map/ppermute | solution.py:14
  16.0 2.5 collective-permute-start.1
  18.5 115.0 %while.28 = (s32[]{:T(128)}, f32[128,2,128]{0,2,1:T(8,128)S(1)}, f32[4,2,128,128]{3,2,1,0:T(8,128)S(1)}, f32[4,2,128,128]{3,2,1,0:T(8,128)}, bf16[2,128,128]{2,1...) while((s32[]{:T(128)}, f32[128,2,128]{0,2,1:T(8,128)S(1)}, ...), condition=%wide.region_2.3_spmd.clone, body=%wide.region_0.2_spmd.clone.sunk | while | flops 336887808 | bytes 7536771 | solution.py:75
  18.5 1.7 fusion.64
  20.2 1.1 copy.110
  21.3 13.4 %all-to-all-start.1 = ((bf16[4,2,2,128,128]{4,1,2,0,3:T(2,128)(2,1)}), bf16[4,2,2,128,128]{4,1,2,0,3:T(2,128)(2,1)S(1)}, u32[]{:S(2)}, u32[]{:S(2)}) async-start(bf16[4,2,2,128,128]{4,1,2,0,3:T(2,128)(2,1)} %copy.110), calls=%async_computation.1 | async-start | bytes 1048576 | tf_op jit(solution)/shard_map/while/body/eval_jaxpr/all_to_all | solution.py:71
  34.7 20.9 %all-to-all-done.1 = bf16[4,2,2,128,128]{4,1,2,0,3:T(2,128)(2,1)S(1)} async-done(((bf16[4,2,2,128,128]{4,1,2,0,3:T(2,128)(2,1)}), bf16[4,2,2,128,128]{4,1,2,0,3:T(2,128)(2,1)S(1)}, u32[]{:S(2)}, u32[]{:S(2)}) %all-to-all-start.1) | async-done | bytes 524320 | tf_op jit(solution)/shard_map/while/body/eval_jaxpr/all_to_all | solution.py:71
  55.7 0.5 copy.112
  56.7 1.7 fusion.64
  58.4 1.1 copy.110
  59.5 4.6 %all-to-all-start.1 = ((bf16[4,2,2,128,128]{4,1,2,0,3:T(2,128)(2,1)}), bf16[4,2,2,128,128]{4,1,2,0,3:T(2,128)(2,1)S(1)}, u32[]{:S(2)}, u32[]{:S(2)}) async-start(bf16[4,2,2,128,128]{4,1,2,0,3:T(2,128)(2,1)} %copy.110), calls=%async_computation.1 | async-start | bytes 1048576 | tf_op jit(solution)/shard_map/while/body/eval_jaxpr/all_to_all | solution.py:71
  64.2 16.9 %all-to-all-done.1 = bf16[4,2,2,128,128]{4,1,2,0,3:T(2,128)(2,1)S(1)} async-done(((bf16[4,2,2,128,128]{4,1,2,0,3:T(2,128)(2,1)}), bf16[4,2,2,128,128]{4,1,2,0,3:T(2,128)(2,1)S(1)}, u32[]{:S(2)}, u32[]{:S(2)}) %all-to-all-start.1) | async-done | bytes 524320 | tf_op jit(solution)/shard_map/while/body/eval_jaxpr/all_to_all | solution.py:71
  81.2 0.5 copy.112
  82.2 1.7 fusion.64
  83.9 1.1 copy.110
  85.0 6.4 %all-to-all-start.1 = ((bf16[4,2,2,128,128]{4,1,2,0,3:T(2,128)(2,1)}), bf16[4,2,2,128,128]{4,1,2,0,3:T(2,128)(2,1)S(1)}, u32[]{:S(2)}, u32[]{:S(2)}) async-start(bf16[4,2,2,128,128]{4,1,2,0,3:T(2,128)(2,1)} %copy.110), calls=%async_computation.1 | async-start | bytes 1048576 | tf_op jit(solution)/shard_map/while/body/eval_jaxpr/all_to_all | solution.py:71
  91.4 15.6 %all-to-all-done.1 = bf16[4,2,2,128,128]{4,1,2,0,3:T(2,128)(2,1)S(1)} async-done(((bf16[4,2,2,128,128]{4,1,2,0,3:T(2,128)(2,1)}), bf16[4,2,2,128,128]{4,1,2,0,3:T(2,128)(2,1)S(1)}, u32[]{:S(2)}, u32[]{:S(2)}) %all-to-all-start.1) | async-done | bytes 524320 | tf_op jit(solution)/shard_map/while/body/eval_jaxpr/all_to_all | solution.py:71
  107.2 0.5 copy.112
  108.2 1.7 fusion.64
  109.8 1.1 copy.110
  111.0 6.2 %all-to-all-start.1 = ((bf16[4,2,2,128,128]{4,1,2,0,3:T(2,128)(2,1)}), bf16[4,2,2,128,128]{4,1,2,0,3:T(2,128)(2,1)S(1)}, u32[]{:S(2)}, u32[]{:S(2)}) async-start(bf16[4,2,2,128,128]{4,1,2,0,3:T(2,128)(2,1)} %copy.110), calls=%async_computation.1 | async-start | bytes 1048576 | tf_op jit(solution)/shard_map/while/body/eval_jaxpr/all_to_all | solution.py:71
  117.2 15.2 %all-to-all-done.1 = bf16[4,2,2,128,128]{4,1,2,0,3:T(2,128)(2,1)S(1)} async-done(((bf16[4,2,2,128,128]{4,1,2,0,3:T(2,128)(2,1)}), bf16[4,2,2,128,128]{4,1,2,0,3:T(2,128)(2,1)S(1)}, u32[]{:S(2)}, u32[]{:S(2)}) %all-to-all-start.1) | async-done | bytes 524320 | tf_op jit(solution)/shard_map/while/body/eval_jaxpr/all_to_all | solution.py:71
  132.6 0.5 copy.112
  133.5 93.3 %while.27 = (s32[]{:T(128)}, f32[128,2,128]{0,2,1:T(8,128)S(1)}, f32[4,2,128,128]{3,2,1,0:T(8,128)S(1)}, f32[4,2,128,128]{3,2,1,0:T(8,128)S(1)}, bf16[2,128,128]...) while((s32[]{:T(128)}, f32[128,2,128]{0,2,1:T(8,128)S(1)}, ...), condition=%wide.region_5.6_spmd, body=%wide.region_3.5_spmd.sunk | while | flops 336855040 | bytes 7536753 | solution.py:75
  133.6 0.6 fusion.57
  134.2 1.1 copy.106
  135.3 5.0 %all-to-all-start = ((bf16[4,2,2,128,128]{4,1,2,0,3:T(2,128)(2,1)}), bf16[4,2,2,128,128]{4,1,2,0,3:T(2,128)(2,1)S(1)}, u32[]{:S(2)}, u32[]{:S(2)}) async-start(bf16[4,2,2,128,128]{4,1,2,0,3:T(2,128)(2,1)} %copy.106), calls=%async_computation | async-start | bytes 1048576 | tf_op jit(solution)/shard_map/while/body/eval_jaxpr/all_to_all | solution.py:71
  140.4 15.6 %all-to-all-done = bf16[4,2,2,128,128]{4,1,2,0,3:T(2,128)(2,1)S(1)} async-done(((bf16[4,2,2,128,128]{4,1,2,0,3:T(2,128)(2,1)}), bf16[4,2,2,128,128]{4,1,2,0,3:T(2,128)(2,1)S(1)}, u32[]{:S(2)}, u32[]{:S(2)}) %all-to-all-start) | async-done | bytes 524320 | tf_op jit(solution)/shard_map/while/body/eval_jaxpr/all_to_all | solution.py:71
  157.1 0.6 fusion.57
  157.7 1.1 copy.106
  158.9 4.6 %all-to-all-start = ((bf16[4,2,2,128,128]{4,1,2,0,3:T(2,128)(2,1)}), bf16[4,2,2,128,128]{4,1,2,0,3:T(2,128)(2,1)S(1)}, u32[]{:S(2)}, u32[]{:S(2)}) async-start(bf16[4,2,2,128,128]{4,1,2,0,3:T(2,128)(2,1)} %copy.106), calls=%async_computation | async-start | bytes 1048576 | tf_op jit(solution)/shard_map/while/body/eval_jaxpr/all_to_all | solution.py:71
  163.5 16.0 %all-to-all-done = bf16[4,2,2,128,128]{4,1,2,0,3:T(2,128)(2,1)S(1)} async-done(((bf16[4,2,2,128,128]{4,1,2,0,3:T(2,128)(2,1)}), bf16[4,2,2,128,128]{4,1,2,0,3:T(2,128)(2,1)S(1)}, u32[]{:S(2)}, u32[]{:S(2)}) %all-to-all-start) | async-done | bytes 524320 | tf_op jit(solution)/shard_map/while/body/eval_jaxpr/all_to_all | solution.py:71
  180.7 0.6 fusion.57
  181.3 1.1 copy.106
  182.4 4.6 %all-to-all-start = ((bf16[4,2,2,128,128]{4,1,2,0,3:T(2,128)(2,1)}), bf16[4,2,2,128,128]{4,1,2,0,3:T(2,128)(2,1)S(1)}, u32[]{:S(2)}, u32[]{:S(2)}) async-start(bf16[4,2,2,128,128]{4,1,2,0,3:T(2,128)(2,1)} %copy.106), calls=%async_computation | async-start | bytes 1048576 | tf_op jit(solution)/shard_map/while/body/eval_jaxpr/all_to_all | solution.py:71
  187.1 16.0 %all-to-all-done = bf16[4,2,2,128,128]{4,1,2,0,3:T(2,128)(2,1)S(1)} async-done(((bf16[4,2,2,128,128]{4,1,2,0,3:T(2,128)(2,1)}), bf16[4,2,2,128,128]{4,1,2,0,3:T(2,128)(2,1)S(1)}, u32[]{:S(2)}, u32[]{:S(2)}) %all-to-all-start) | async-done | bytes 524320 | tf_op jit(solution)/shard_map/while/body/eval_jaxpr/all_to_all | solution.py:71
  204.2 0.6 fusion.57
  204.8 1.1 copy.106
  206.0 4.6 %all-to-all-start = ((bf16[4,2,2,128,128]{4,1,2,0,3:T(2,128)(2,1)}), bf16[4,2,2,128,128]{4,1,2,0,3:T(2,128)(2,1)S(1)}, u32[]{:S(2)}, u32[]{:S(2)}) async-start(bf16[4,2,2,128,128]{4,1,2,0,3:T(2,128)(2,1)} %copy.106), calls=%async_computation | async-start | bytes 1048576 | tf_op jit(solution)/shard_map/while/body/eval_jaxpr/all_to_all | solution.py:71
  210.6 15.2 %all-to-all-done = bf16[4,2,2,128,128]{4,1,2,0,3:T(2,128)(2,1)S(1)} async-done(((bf16[4,2,2,128,128]{4,1,2,0,3:T(2,128)(2,1)}), bf16[4,2,2,128,128]{4,1,2,0,3:T(2,128)(2,1)S(1)}, u32[]{:S(2)}, u32[]{:S(2)}) %all-to-all-start) | async-done | bytes 524320 | tf_op jit(solution)/shard_map/while/body/eval_jaxpr/all_to_all | solution.py:71
  227.0 16.2 %all_to_all.86 = f32[128,2,128]{2,1,0:T(2,128)S(1)} all-to-all(f32[128,2,128]{2,1,0:T(2,128)S(1)} %copy.65), channel_id=1, replica_groups=mesh['band'=4,'slab'=64] {'slab'}, dimensions={0} | all-to-all | bytes 262144 | tf_op jit(solution)/shard_map/all_to_all | solution.py:76
  243.3 0.8 copy.68
  244.1 0.7 copy-done.1
  244.7 0.6 dynamic-slice
  246.0 44.1 %all-reduce.3.cloned.1.call-done = f32[2,128,128]{1,0,2:T(2,128)} async-done(((f32[2,128,128]{1,0,2:T(2,128)}), f32[2,128,128]{1,0,2:T(2,128)}) %all-reduce.3.cloned.1.call-update) | async-done | bytes 131088
  290.1 0.8 constant_dynamic-slice_fusion
  290.8 0.6 copy_multiply_fusion
  (50 shorter events, 7.2 us)
Async XLA Ops:
  6.5 12.0 %copy-start = (f32[4,2,128,128]{3,2,1,0:T(8,128)S(1)}, f32[4,2,128,128]{3,2,1,0:T(8,128)}, u32[]{:S(2)}) copy-start(f32[4,2,128,128]{3,2,1,0:T(8,128)} %param.5) | copy-start | bytes 1572868
  6.5 283.5 %all-reduce.3.cloned.1.call-start = ((), (), s32[]{:S(2)}) async-start(), calls=%async_computation.3 | async-start | bytes 262144
  6.5 9.5 %collective-permute-start = (f32[4,2,128,128]{3,2,1,0:T(8,128)}, f32[4,2,128,128]{3,2,1,0:T(8,128)}, u32[]{:S(2)}, u32[]{:S(2)}) collective-permute-start(f32[4,2,128,128]{3,2,1,0:T(8,128)} %param.5), channel_id=1, source_target_pairs={{0,64},{64,128},{128,192},{192,0},{1,65},{65,129},{129,193},{193,1... | collective-permute-start | bytes 1572872 | tf_op jit(solution)/shard_map/ppermute | solution.py:14
  16.0 117.5 %collective-permute-start.1 = (f32[4,2,128,128]{3,2,1,0:T(8,128)}, f32[4,2,128,128]{3,2,1,0:T(8,128)S(1)}, u32[]{:S(2)}, u32[]{:S(2)}) collective-permute-start(f32[4,2,128,128]{3,2,1,0:T(8,128)} %collective-permute-done), channel_id=1, source_target_pairs={{0,64},{64,128},{128,192},{192,0},{1,65},{65,129},{129,193},{193,1... | collective-permute-start | bytes 1572872 | tf_op jit(solution)/shard_map/ppermute | solution.py:14
  21.3 34.3 %all-to-all-start.1 = ((bf16[4,2,2,128,128]{4,1,2,0,3:T(2,128)(2,1)}), bf16[4,2,2,128,128]{4,1,2,0,3:T(2,128)(2,1)S(1)}, u32[]{:S(2)}, u32[]{:S(2)}) async-start(bf16[4,2,2,128,128]{4,1,2,0,3:T(2,128)(2,1)} %copy.110), calls=%async_computation.1 | async-start | bytes 1048576 | tf_op jit(solution)/shard_map/while/body/eval_jaxpr/all_to_all | solution.py:71
  59.5 21.5 %all-to-all-start.1 = ((bf16[4,2,2,128,128]{4,1,2,0,3:T(2,128)(2,1)}), bf16[4,2,2,128,128]{4,1,2,0,3:T(2,128)(2,1)S(1)}, u32[]{:S(2)}, u32[]{:S(2)}) async-start(bf16[4,2,2,128,128]{4,1,2,0,3:T(2,128)(2,1)} %copy.110), calls=%async_computation.1 | async-start | bytes 1048576 | tf_op jit(solution)/shard_map/while/body/eval_jaxpr/all_to_all | solution.py:71
  85.0 22.1 %all-to-all-start.1 = ((bf16[4,2,2,128,128]{4,1,2,0,3:T(2,128)(2,1)}), bf16[4,2,2,128,128]{4,1,2,0,3:T(2,128)(2,1)S(1)}, u32[]{:S(2)}, u32[]{:S(2)}) async-start(bf16[4,2,2,128,128]{4,1,2,0,3:T(2,128)(2,1)} %copy.110), calls=%async_computation.1 | async-start | bytes 1048576 | tf_op jit(solution)/shard_map/while/body/eval_jaxpr/all_to_all | solution.py:71
  111.0 21.4 %all-to-all-start.1 = ((bf16[4,2,2,128,128]{4,1,2,0,3:T(2,128)(2,1)}), bf16[4,2,2,128,128]{4,1,2,0,3:T(2,128)(2,1)S(1)}, u32[]{:S(2)}, u32[]{:S(2)}) async-start(bf16[4,2,2,128,128]{4,1,2,0,3:T(2,128)(2,1)} %copy.110), calls=%async_computation.1 | async-start | bytes 1048576 | tf_op jit(solution)/shard_map/while/body/eval_jaxpr/all_to_all | solution.py:71
  135.3 20.7 %all-to-all-start = ((bf16[4,2,2,128,128]{4,1,2,0,3:T(2,128)(2,1)}), bf16[4,2,2,128,128]{4,1,2,0,3:T(2,128)(2,1)S(1)}, u32[]{:S(2)}, u32[]{:S(2)}) async-start(bf16[4,2,2,128,128]{4,1,2,0,3:T(2,128)(2,1)} %copy.106), calls=%async_computation | async-start | bytes 1048576 | tf_op jit(solution)/shard_map/while/body/eval_jaxpr/all_to_all | solution.py:71
  158.9 20.7 %all-to-all-start = ((bf16[4,2,2,128,128]{4,1,2,0,3:T(2,128)(2,1)}), bf16[4,2,2,128,128]{4,1,2,0,3:T(2,128)(2,1)S(1)}, u32[]{:S(2)}, u32[]{:S(2)}) async-start(bf16[4,2,2,128,128]{4,1,2,0,3:T(2,128)(2,1)} %copy.106), calls=%async_computation | async-start | bytes 1048576 | tf_op jit(solution)/shard_map/while/body/eval_jaxpr/all_to_all | solution.py:71
  182.4 20.7 %all-to-all-start = ((bf16[4,2,2,128,128]{4,1,2,0,3:T(2,128)(2,1)}), bf16[4,2,2,128,128]{4,1,2,0,3:T(2,128)(2,1)S(1)}, u32[]{:S(2)}, u32[]{:S(2)}) async-start(bf16[4,2,2,128,128]{4,1,2,0,3:T(2,128)(2,1)} %copy.106), calls=%async_computation | async-start | bytes 1048576 | tf_op jit(solution)/shard_map/while/body/eval_jaxpr/all_to_all | solution.py:71
  206.0 19.8 %all-to-all-start = ((bf16[4,2,2,128,128]{4,1,2,0,3:T(2,128)(2,1)}), bf16[4,2,2,128,128]{4,1,2,0,3:T(2,128)(2,1)S(1)}, u32[]{:S(2)}, u32[]{:S(2)}) async-start(bf16[4,2,2,128,128]{4,1,2,0,3:T(2,128)(2,1)} %copy.106), calls=%async_computation | async-start | bytes 1048576 | tf_op jit(solution)/shard_map/while/body/eval_jaxpr/all_to_all | solution.py:71
  244.0 0.7 copy-start.1
Sparse Core Ops, SparseCore 0:
  244.2 45.8 all-reduce.2
where the time goes:
time: 299 us; the launch traced here: 298 us
  waiting for transfers between devices  181 us (61%)
  starting transfers between devices  55.1 us (18%)
  local copies, waits for them, and re-layouts  17.6 us (6%)
  blocking collectives  16.2 us (5%)
  between operations  14.1 us (5%)
  matrix products  11.8 us (4%)
    all_to_all x8, waiting for transfers between devices, some_orbitals(): lax.all_to_all(second_pass, 'slab', split_axis=3, concat_axis=2, tiled=True)  131 us
    all_to_all x8, starting transfers between devices, some_orbitals(): lax.all_to_all(second_pass, 'slab', split_axis=3, concat_axis=2, tiled=True)  49.6 us
    unnamed x2, waiting for transfers between devices  44.1 us
    all_to_all x1, blocking collectives, local(): lax.all_to_all(accumulated, 'slab', split_axis=0, concat_axis=1, tiled=True)  16.2 us
    convert_element_type x8, local copies, waits for them, and re-layouts, two_passes(): return jnp.einsum('pcxyz,dcky->pdxkz', first_pass, complex_table, preferr...  9.11 us
    dot_general x8, matrix products, two_passes(): jnp.einsum('pcxyz,dcky->pdxkz', first_pass, complex_table, preferred_elem...  9.06 us
  transfers between devices with their start and end apart: 11, of which 10 were waited for; matrix products, arithmetic and copies ran while one was open for 6% of the time, Pallas kernels for 0%

commit v1 on v0

v1 whole, which is shorter than its diff:
```python
import functools
import math

import jax
import jax.numpy as jnp
import ml_dtypes
import numpy as np
from jax import lax
from jax.experimental import pallas as pl
from jax.experimental.pallas import tpu as pltpu
from jax.sharding import PartitionSpec as P

MESH = pl.DeviceIdType.MESH
NG = 128
BF16 = ml_dtypes.bfloat16
EDGES = ((0, 1, 1.0), (1, 2, 1.0), (0, 2, 2.0))


def ky_order():
    rows = [0, 64, 1, 127]
    for d in range(1, 32):
        rows += [2 * d, 128 - 2 * d, 2 * d + 1, 127 - 2 * d]
    return np.array(rows)


def kx_order():
    return np.array([8 * yx + 2 * zh + e for zh in range(4) for e in range(2) for yx in range(16)])


def tables():
    n = np.arange(NG)
    angle = ((n[:, None] * n[None]) % NG).astype(np.float32) * np.float32(2.0 * math.pi / NG)
    factor = np.float32(1.0 / math.sqrt(NG))
    c = (np.cos(angle) * factor).astype(BF16).astype(np.float32)
    s = (-np.sin(angle) * factor).astype(BF16).astype(np.float32)
    ky, kx = ky_order(), kx_order()
    first = np.block([[c.T, s.T], [-s.T, c.T]])
    second = np.block([[c[ky], -s[ky]], [s[ky], c[ky]]])
    third = np.zeros((2, 2, NG, 32, 2, 2, 4), np.float32)
    src, x4 = np.arange(32)[:, None], np.arange(4)[None]
    x_global = (src // 2) * 8 + x4 * 2 + src % 2
    cx, sx = c[kx][:, x_global], s[kx][:, x_global]
    for q in range(2):
        third[q, 0, :, :, q, 0] = cx
        third[q, 0, :, :, q, 1] = -sx
        third[q, 1, :, :, q, 0] = sx
        third[q, 1, :, :, q, 1] = cx
    third = third.reshape(512, 512)
    mirror = ((kx[:, None] + kx[None]) % NG == 0).astype(np.float32)
    spread = np.zeros((2, 4, NG, 4, 4, 32), np.float32)
    partner = (1, 0, 3, 2)
    for slot in range(4):
        for b in range(4):
            for k in range(32):
                kz = 32 * b + k
                spread[0, slot, kz, b, slot, k] = 1
                spread[1, partner[slot], -kz % NG, b, slot, k] = 1
    spread = spread.reshape(1024, 512)
    place = np.zeros((2, 4, NG, NG), np.float32)
    for e in range(2):
        for slot in range(4):
            for d in range(32):
                place[e, slot, ky[d * 4 + slot], (d // 2) * 8 + (d % 2) * 2 + e] = 1
    place = place.reshape(1024, NG)
    return [t.astype(BF16) for t in (first, second, third, mirror, spread, place)]


def dot(a, b):
    return jnp.dot(a, b, preferred_element_type=jnp.float32)


def kernel(
    x_hbm, t1_hbm, t2_hbm, t3_hbm, mir_hbm, spr_hbm, plc_hbm, out_ref,
    x_ref, t1, t2, t3, mir, spr, plc,
    own, orb, prod, first_out, grid_rows, msg, got, power, u_ref, r1, v_ref, s2, r2,
    load_sem, g_send, g_recv, a_send, a_recv, u_send, u_recv, s_send, s_recv,
):
    band, slab = lax.axis_index("band"), lax.axis_index("slab")
    zl, c = lax.div(band, 2), lax.rem(band, 2)
    y, x, zh = lax.div(slab, 16), lax.rem(lax.div(slab, 4), 4), lax.rem(slab, 4)
    z = 2 * zh + zl
    yx = y * 4 + x
    d_me = yx * 2 + c

    def line(z_to, c_to):
        return {"band": lax.rem(z_to, 2) * 2 + c_to, "slab": yx * 4 + lax.div(z_to, 2)}

    def plane(yx_to, c_to):
        return {"band": zl * 2 + c_to, "slab": yx_to * 4 + zh}

    barrier = pltpu.get_barrier_semaphore()

    def greet(to):
        pl.semaphore_signal(barrier, inc=1, device_id=to, device_id_type=MESH)

    def greet_line(i, _):
        greet(line(lax.rem(z + lax.div(i, 2), 8), lax.rem(c + i, 2)))
        return 0

    def plane_peer(i):
        dyx, dc = lax.div(i, 2), lax.rem(i, 2)
        y_to = lax.rem(y + lax.div(dyx, 4), 4)
        x_to = lax.rem(x + lax.rem(dyx, 4), 4)
        return y_to * 4 + x_to, lax.rem(c + dc, 2)

    def greet_plane(i, _):
        greet(plane(*plane_peer(i)))
        return 0

    lax.fori_loop(1, 16, greet_line, 0)
    lax.fori_loop(2, 32, greet_plane, 0)
    loads = []
    for i, (a, b) in enumerate(
        ((x_hbm, x_ref), (t1_hbm, t1), (t2_hbm, t2), (t3_hbm, t3), (mir_hbm, mir), (spr_hbm, spr), (plc_hbm, plc))
    ):
        loads.append(pltpu.make_async_copy(a, b, load_sem.at[i]))
        loads[-1].start()
    loads[0].wait()
    for e in range(2):
        own[e] = x_ref[:, e].astype(jnp.bfloat16)
    v_ref[...] = jnp.zeros_like(v_ref)
    pl.semaphore_wait(barrier, 45)

    def gather_parts(j, p, c_to):
        m = lax.rem(band + 3 - j, 4)
        twist = (1 - lax.rem(m, 2)) * c + lax.rem(m + lax.div(m, 2), 2) * zl
        h = lax.rem(p + twist, 2)
        z_to = 2 * (2 * p + lax.rem(m, 2)) + 1 - lax.div(m, 2)
        src = own.at[c_to, pl.ds(2 * h, 2)]
        dst = orb.at[j, zh]
        here = jnp.logical_and(z_to == z, c_to == c)
        i = j * 4 + p * 2 + c_to

        def local_copy():
            return pltpu.make_async_copy(src, dst, g_recv.at[j, zh])

        def far_copy():
            return pltpu.make_async_remote_copy(
                src, dst, g_send.at[i], g_recv.at[j, zh], device_id=line(z_to, c_to), device_id_type=MESH
            )

        return here, local_copy, far_copy

    for j in range(3):
        for p in range(2):
            for c_to in range(2):
                here, local_copy, far_copy = gather_parts(j, p, c_to)
                pl.when(here)(lambda: local_copy().start())
                pl.when(jnp.logical_not(here))(lambda: far_copy().start())

    def wait_slot(j):
        for k in range(4):
            pltpu.make_async_copy(orb.at[j, k], orb.at[j, k], g_recv.at[j, k]).wait()

    def exchange(g, i):
        yx_to, c_to = plane_peer(i)
        d_to = yx_to * 2 + c_to
        return pltpu.make_async_remote_copy(
            msg.at[g, d_to], got.at[g, :, pl.ds(pl.multiple_of(d_me * 16, 16), 16)],
            a_send.at[g, i], a_recv.at[g], device_id=plane(yx_to, c_to), device_id_type=MESH,
        )

    loads[1].wait()
    loads[2].wait()
    for g, (ja, jb, _) in enumerate(EDGES):
        if g == 0:
            wait_slot(0)
            wait_slot(1)
        elif g == 1:
            wait_slot(2)

        def one_q(q, _):
            for k in range(4):
                left = orb[ja, k, q]
                for part in range(2):
                    prod[pl.ds(k * NG, NG), pl.ds(part * NG, NG)] = left * orb[jb, k, part]
            first_out[...] = dot(prod[...], t1[...]).astype(jnp.bfloat16)
            for k in range(4):
                rows = first_out[pl.ds(k * NG, NG), :]
                stacked = jnp.concatenate([rows[:, :NG], rows[:, NG:]], axis=0)
                second = dot(t2[...], stacked)
                grid_rows[q, pl.ds(k * NG, NG), :] = second[:NG]
                grid_rows[q, pl.ds((4 + k) * NG, NG), :] = second[NG:]
            return 0

        lax.fori_loop(0, 2, one_q, 0)

        def turn(d, _):
            for slot in range(4):
                halves = [grid_rows[q, pl.ds(d * 4 + slot, 8, stride=NG), :] for q in range(2)]
                msg[g, d, slot] = jnp.concatenate(halves, axis=0).astype(jnp.bfloat16)
            return 0

        lax.fori_loop(0, 32, turn, 0)

        def send(i, _):
            exchange(g, i).start()
            return 0

        lax.fori_loop(1, 32, send, 0)
        pltpu.make_async_copy(
            msg.at[g, d_me], got.at[g, :, pl.ds(pl.multiple_of(d_me * 16, 16), 16)], a_recv.at[g]
        ).start()

    loads[3].wait()
    for g, (_, _, weight) in enumerate(EDGES):
        pltpu.make_async_copy(got.at[g], got.at[g], a_recv.at[g]).wait()

        def one_ky(slot, _):
            f = dot(t3[...], got[g, slot])
            total = f[:128] * f[:128] + f[128:256] * f[128:256] + f[256:384] * f[256:384] + f[384:] * f[384:]
            if g == 0:
                power[slot] = total
            else:
                power[slot] += total * weight
            return 0

        lax.fori_loop(0, 4, one_ky, 0)

    loads[4].wait()
    loads[5].wait()
    direct = jnp.concatenate([power[i] for i in range(4)], axis=1).astype(jnp.bfloat16)
    flipped = dot(mir[...], direct).astype(jnp.bfloat16)
    f0, f1 = flipped[:, :128], flipped[:, 128:256]
    alone = d_me == 0
    flipped = jnp.concatenate([jnp.where(alone, f1, f0), jnp.where(alone, f0, f1), flipped[:, 256:]], axis=1)
    both = (dot(direct, spr[:512]) + dot(flipped, spr[512:])) * (1.0 / 256.0)
    for a in range(4):
        for b in range(4):
            u_ref[a, b] = both[a * 32 : a * 32 + 32, b * 128 : b * 128 + 128].astype(jnp.bfloat16)

    def reduce_copy(i):
        z_to, c_to = lax.rem(z + lax.div(i, 2), 8), lax.rem(c + i, 2)
        return pltpu.make_async_remote_copy(
            u_ref.at[lax.div(z_to, 2), lax.rem(z_to, 2) * 2 + c_to], r1.at[z * 2 + c],
            u_send.at[i], u_recv, device_id=line(z_to, c_to), device_id_type=MESH,
        )

    def reduce_send(i, _):
        reduce_copy(i).start()
        return 0

    lax.fori_loop(1, 16, reduce_send, 0)
    pltpu.make_async_copy(u_ref.at[zh, band], r1.at[z * 2 + c], u_recv).start()
    pltpu.make_async_copy(r1, r1, u_recv).wait()
    for cs in range(2):
        total = r1[cs].astype(jnp.float32)
        for k in range(1, 8):
            total += r1[2 * k + cs].astype(jnp.float32)
        v_ref[pl.ds(cs * 32, 32), :] = total
    for k in range(16):
        s2[k] = v_ref[pl.ds(k, 8, stride=16), :]

    def owner_copy(i):
        yx_to, c_to = plane_peer(2 * i)
        return pltpu.make_async_remote_copy(
            s2.at[yx_to], r2.at[yx], s_send.at[i], s_recv, device_id=plane(yx_to, c_to), device_id_type=MESH
        )

    def owner_send(i, _):
        owner_copy(i).start()
        return 0

    lax.fori_loop(1, 16, owner_send, 0)
    pltpu.make_async_copy(s2.at[yx], r2.at[yx], s_recv).start()
    loads[6].wait()
    pltpu.make_async_copy(r2, r2, s_recv).wait()
    rows = r2[...].reshape(128, 128)
    high = rows.astype(jnp.bfloat16)
    low = (rows - high.astype(jnp.float32)).astype(jnp.bfloat16)
    placed = dot(plc[...], high) + dot(plc[...], low)
    for e in range(2):
        total = None
        for slot in range(4):
            part = placed[(e * 4 + slot) * 128 : (e * 4 + slot + 1) * 128, slot * 32 : slot * 32 + 32]
            total = part if total is None else total + part
        out_ref[e] = total

    for j in range(3):
        for p in range(2):
            for c_to in range(2):
                here, _, far_copy = gather_parts(j, p, c_to)
                pl.when(jnp.logical_not(here))(lambda: far_copy().wait_send())
    for g in range(3):

        def sent(i, _):
            exchange(g, i).wait_send()
            return 0

        lax.fori_loop(1, 32, sent, 0)

    def sent_small(i, _):
        reduce_copy(i).wait_send()
        owner_copy(i).wait_send()
        return 0

    lax.fori_loop(1, 16, sent_small, 0)


def solution(mesh):
    consts = tables()
    vm, bf, f32 = pltpu.VMEM, jnp.bfloat16, jnp.float32

    def local(orbitals):
        return pl.pallas_call(
            kernel,
            out_shape=jax.ShapeDtypeStruct((2, NG, 32), f32),
            in_specs=[pl.BlockSpec(memory_space=pl.ANY)] * 7,
            out_specs=pl.BlockSpec(memory_space=pltpu.VMEM),
            scratch_shapes=[
                vm((4, 2, NG, NG), f32),
                vm((256, 256), bf), vm((256, 256), bf), vm((512, 512), bf),
                vm((128, 128), bf), vm((1024, 512), bf), vm((1024, 128), bf),
                vm((2, 4, NG, NG), bf),
                vm((3, 4, 2, NG, NG), bf),
                vm((512, 256), bf),
                vm((512, 256), bf),
                vm((2, 1024, 128), f32),
                vm((3, 32, 4, 16, 128), bf),
                vm((3, 4, 512, 128), bf),
                vm((4, 128, 128), f32),
                vm((4, 4, 32, 128), bf),
                vm((16, 32, 128), bf),
                vm((128, 128), f32),
                vm((16, 8, 128), f32),
                vm((16, 8, 128), f32),
                pltpu.SemaphoreType.DMA((7,)),
                pltpu.SemaphoreType.DMA((12,)),
                pltpu.SemaphoreType.DMA((3, 4)),
                pltpu.SemaphoreType.DMA((3, 32)),
                pltpu.SemaphoreType.DMA((3,)),
                pltpu.SemaphoreType.DMA((16,)),
                pltpu.SemaphoreType.DMA,
                pltpu.SemaphoreType.DMA((16,)),
                pltpu.SemaphoreType.DMA,
            ],
            compiler_params=pltpu.CompilerParams(collective_id=0, has_side_effects=True),
        )(orbitals, *[jnp.asarray(t) for t in consts])

    return jax.shard_map(
        local,
        mesh=mesh,
        in_specs=(P("band", "slab", None, None),),
        out_specs=P("slab", None, "band"),
        check_vma=False,
    )
```

time: 299 us -> 64 us (0.21)
  waiting for transfers between devices: 181 us -> 0 us
  Pallas kernels: 0 us -> 62.3 us
  starting transfers between devices: 55.1 us -> 0 us
  blocking collectives: 16.2 us -> 0 us
  local copies, waits for them, and re-layouts: 17.6 us -> 1.59 us
  between operations: 14.1 us -> 0.01 us
  matrix products: 11.8 us -> 0 us
    all_to_all x8 -> x0, waiting for transfers between devices: 131 us -> none  [some_orbitals(): lax.all_to_all(second_pass, 'slab', split_axis=3, concat_axis=2, tiled=True)]
    pallas_call x0 -> x1, Pallas kernels: none -> 62.3 us  [local(): pl.pallas_call(kernel, out_shape=jax.ShapeDtypeStruct((2, NG, 32), f32),...]
    all_to_all x8 -> x0, starting transfers between devices: 49.6 us -> none  [some_orbitals(): lax.all_to_all(second_pass, 'slab', split_axis=3, concat_axis=2, tiled=True)]
    unnamed x2 -> x0, waiting for transfers between devices: 44.1 us -> none
    all_to_all x1 -> x0, blocking collectives: 16.2 us -> none  [local(): lax.all_to_all(accumulated, 'slab', split_axis=0, concat_axis=1, tiled=True)]
    dot_general x16 -> x0, matrix products: 11.8 us -> none  [the longest x8 9.06 us: two_passes(): jnp.einsum('pcxyz,dcky->pdxkz', first_pass, complex_table, preferred_elem...]
    convert_element_type x8 -> x0, local copies, waits for them, and re-layouts: 9.11 us -> none  [two_passes(): return jnp.einsum('pcxyz,dcky->pdxkz', first_pass, complex_table, preferr...]
    all_to_all x19 -> x0, local copies, waits for them, and re-layouts: 6.29 us -> none  [the longest x16 5.42 us: some_orbitals(): lax.all_to_all(second_pass, 'slab', split_axis=3, concat_axis=2, tiled=True)]
  transfers between devices with their start and end apart: 11 -> 0, of which waited for: 10 -> 0; matrix products, arithmetic and copies ran while one was open for 6% -> 0% of each run, Pallas kernels for 0% -> 0%
where the time goes in v1:
time: 64 us; the launch traced here: 63.9 us
  Pallas kernels  62.3 us (97%)
  local copies, waits for them, and re-layouts  1.59 us (2%)
    pallas_call x1, Pallas kernels, local(): pl.pallas_call(kernel, out_shape=jax.ShapeDtypeStruct((2, NG, 32), f32),...  62.3 us
    pallas_call x1, local copies, waits for them, and re-layouts, local(): pl.pallas_call(kernel, out_shape=jax.ShapeDtypeStruct((2, NG, 32), f32),...  1.59 us

profile of v1, /device:TPU:1, one launch (start us, length us, event | category | flops | bytes accessed | tf_op | source)
XLA Modules:
  0.0 63.9 jit_solution(13213153985721150876)
XLA Ops:
  0.0 62.3 %shard_map.73 = f32[2,128,32]{2,1,0:T(8,128)} custom-call(f32[4,2,128,128]{3,2,1,0:T(8,128)} %x_hbm.1, bf16[256,256]{1,0:T(8,128)(2,1)} %constant.12.clone.t1_hbm, bf16[256,256]{1,0:T(8,128)(2,1)} %constant.13.clone.t2_hbm, bf16[512,512]{1,0:T(8,128)(2,1)} %constant.14.clone.t3_hbm, bf16[128,128]{1,0:T(8,128)(2,1)} %constant.15.clone.mir_hbm, ...), custom_call_target="tpu_custom_call" | custom-call | tf_op jit(solution)/shard_map/pallas_call | solution.py:305
  62.3 1.6 %copy.8 = f32[2,128,32]{1,2,0:T(8,128)} copy(f32[2,128,32]{2,1,0:T(8,128)} %shard_map.73) | data formatting | bytes 65536 | tf_op jit(solution)/shard_map/pallas_call | solution.py:305

commit v2 on v1

--- a/solution.py
+++ b/solution.py
@@ -13,7 +13,8 @@
 MESH = pl.DeviceIdType.MESH
 NG = 128
 BF16 = ml_dtypes.bfloat16
-EDGES = ((0, 1, 1.0), (1, 2, 1.0), (0, 2, 2.0))
+PIECES = ((0, 0), (1, 0), (1, 1), (0, 1), (2, 0), (2, 1))
+UNITS = ((3, 0, 0, 1, 1.0), (4, 0, 1, 1, 1.0), (5, 2, 0, 1, 1.0), (5, 2, 0, 0, 2.0), (6, 2, 1, 1, 1.0), (6, 2, 1, 0, 2.0))
 
 
 def ky_order():
@@ -121,77 +122,72 @@
     v_ref[...] = jnp.zeros_like(v_ref)
     pl.semaphore_wait(barrier, 45)
 
-    def gather_parts(j, p, c_to):
+    def gather_parts(n, p, c_to):
+        j, o = PIECES[n]
         m = lax.rem(band + 3 - j, 4)
         twist = (1 - lax.rem(m, 2)) * c + lax.rem(m + lax.div(m, 2), 2) * zl
         h = lax.rem(p + twist, 2)
         z_to = 2 * (2 * p + lax.rem(m, 2)) + 1 - lax.div(m, 2)
-        src = own.at[c_to, pl.ds(2 * h, 2)]
-        dst = orb.at[j, zh]
+        src = own.at[c_to, 2 * h + o]
+        dst = orb.at[j, zh, o]
         here = jnp.logical_and(z_to == z, c_to == c)
-        i = j * 4 + p * 2 + c_to
 
         def local_copy():
-            return pltpu.make_async_copy(src, dst, g_recv.at[j, zh])
+            return pltpu.make_async_copy(src, dst, g_recv.at[n, zh])
 
         def far_copy():
             return pltpu.make_async_remote_copy(
-                src, dst, g_send.at[i], g_recv.at[j, zh], device_id=line(z_to, c_to), device_id_type=MESH
+                src, dst, g_send.at[n, p * 2 + c_to], g_recv.at[n, zh], device_id=line(z_to, c_to), device_id_type=MESH
             )
 
         return here, local_copy, far_copy
 
-    for j in range(3):
+    for n in range(6):
         for p in range(2):
             for c_to in range(2):
-                here, local_copy, far_copy = gather_parts(j, p, c_to)
+                here, local_copy, far_copy = gather_parts(n, p, c_to)
                 pl.when(here)(lambda: local_copy().start())
                 pl.when(jnp.logical_not(here))(lambda: far_copy().start())
 
-    def wait_slot(j):
+    def wait_piece(n):
+        j, o = PIECES[n]
         for k in range(4):
-            pltpu.make_async_copy(orb.at[j, k], orb.at[j, k], g_recv.at[j, k]).wait()
+            pltpu.make_async_copy(orb.at[j, k, o], orb.at[j, k, o], g_recv.at[n, k]).wait()
 
     def exchange(g, i):
         yx_to, c_to = plane_peer(i)
         d_to = yx_to * 2 + c_to
         return pltpu.make_async_remote_copy(
             msg.at[g, d_to], got.at[g, :, pl.ds(pl.multiple_of(d_me * 16, 16), 16)],
-            a_send.at[g, i], a_recv.at[g], device_id=plane(yx_to, c_to), device_id_type=MESH,
+            a_send.at[g], a_recv.at[g], device_id=plane(yx_to, c_to), device_id_type=MESH,
         )
 
     loads[1].wait()
     loads[2].wait()
-    for g, (ja, jb, _) in enumerate(EDGES):
-        if g == 0:
-            wait_slot(0)
-            wait_slot(1)
-        elif g == 1:
-            wait_slot(2)
-
-        def one_q(q, _):
-            for k in range(4):
-                left = orb[ja, k, q]
-                for part in range(2):
-                    prod[pl.ds(k * NG, NG), pl.ds(part * NG, NG)] = left * orb[jb, k, part]
-            first_out[...] = dot(prod[...], t1[...]).astype(jnp.bfloat16)
-            for k in range(4):
-                rows = first_out[pl.ds(k * NG, NG), :]
-                stacked = jnp.concatenate([rows[:, :NG], rows[:, NG:]], axis=0)
-                second = dot(t2[...], stacked)
-                grid_rows[q, pl.ds(k * NG, NG), :] = second[:NG]
-                grid_rows[q, pl.ds((4 + k) * NG, NG), :] = second[NG:]
+    held = 0
+    for g, (needs, jl, ol, jr, _) in enumerate(UNITS):
+        while held < needs:
+            wait_piece(held)
+            held += 1
+        for k in range(4):
+            left = orb[jl, k, ol]
+            for part in range(2):
+                prod[pl.ds(k * NG, NG), pl.ds(part * NG, NG)] = left * orb[jr, k, part]
+        first_out[...] = dot(prod[...], t1[...]).astype(jnp.bfloat16)
+        for k in range(4):
+            rows = first_out[pl.ds(k * NG, NG), :]
+            stacked = jnp.concatenate([rows[:, :NG], rows[:, NG:]], axis=0)
+            second = dot(t2[...], stacked)
+            grid_rows[pl.ds(k * NG, NG), :] = second[:NG]
+            grid_rows[pl.ds((4 + k) * NG, NG), :] = second[NG:]
+
+        def turn(d, _):
+            for pair in range(2):
+                both_ky = [grid_rows[pl.ds(d * 4 + pair * 2 + i, 8, stride=NG), :] for i in range(2)]
+                msg[g, d, pair] = jnp.concatenate(both_ky, axis=0).astype(jnp.bfloat16)
             return 0
 
-        lax.fori_loop(0, 2, one_q, 0)
-
-        def turn(d, _):
-            for slot in range(4):
-                halves = [grid_rows[q, pl.ds(d * 4 + slot, 8, stride=NG), :] for q in range(2)]
-                msg[g, d, slot] = jnp.concatenate(halves, axis=0).astype(jnp.bfloat16)
-            return 0
-
-        lax.fori_loop(0, 32, turn, 0)
+        lax.fori_loop(0, 32, turn, 0, unroll=4)
 
         def send(i, _):
             exchange(g, i).start()
@@ -203,19 +199,17 @@
         ).start()
 
     loads[3].wait()
-    for g, (_, _, weight) in enumerate(EDGES):
+    for g, (_, _, _, _, weight) in enumerate(UNITS):
         pltpu.make_async_copy(got.at[g], got.at[g], a_recv.at[g]).wait()
-
-        def one_ky(slot, _):
-            f = dot(t3[...], got[g, slot])
-            total = f[:128] * f[:128] + f[128:256] * f[128:256] + f[256:384] * f[256:384] + f[384:] * f[384:]
-            if g == 0:
-                power[slot] = total
-            else:
-                power[slot] += total * weight
-            return 0
-
-        lax.fori_loop(0, 4, one_ky, 0)
+        for pair in range(2):
+            f = dot(t3[...], got[g, pair])
+            for i in range(2):
+                re, im = f[i * 256 : i * 256 + 128], f[i * 256 + 128 : i * 256 + 256]
+                total = re * re + im * im
+                if g == 0:
+                    power[pair * 2 + i] = total
+                else:
+                    power[pair * 2 + i] += total * weight
 
     loads[4].wait()
     loads[5].wait()
@@ -233,7 +227,7 @@
         z_to, c_to = lax.rem(z + lax.div(i, 2), 8), lax.rem(c + i, 2)
         return pltpu.make_async_remote_copy(
             u_ref.at[lax.div(z_to, 2), lax.rem(z_to, 2) * 2 + c_to], r1.at[z * 2 + c],
-            u_send.at[i], u_recv, device_id=line(z_to, c_to), device_id_type=MESH,
+            u_send, u_recv, device_id=line(z_to, c_to), device_id_type=MESH,
         )
 
     def reduce_send(i, _):
@@ -242,6 +236,14 @@
 
     lax.fori_loop(1, 16, reduce_send, 0)
     pltpu.make_async_copy(u_ref.at[zh, band], r1.at[z * 2 + c], u_recv).start()
+    for n in range(6):
+        for p in range(2):
+            for c_to in range(2):
+                here, _, far_copy = gather_parts(n, p, c_to)
+                pl.when(jnp.logical_not(here))(lambda: far_copy().wait_send())
+    for g in range(6):
+        pltpu.make_async_copy(msg.at[g, pl.ds(0, 31)], msg.at[g, pl.ds(0, 31)], a_send.at[g]).wait()
+    pltpu.make_async_copy(r1.at[pl.ds(0, 15)], r1.at[pl.ds(0, 15)], u_send).wait()
     pltpu.make_async_copy(r1, r1, u_recv).wait()
     for cs in range(2):
         total = r1[cs].astype(jnp.float32)
@@ -254,7 +256,7 @@
     def owner_copy(i):
         yx_to, c_to = plane_peer(2 * i)
         return pltpu.make_async_remote_copy(
-            s2.at[yx_to], r2.at[yx], s_send.at[i], s_recv, device_id=plane(yx_to, c_to), device_id_type=MESH
+            s2.at[yx_to], r2.at[yx], s_send, s_recv, device_id=plane(yx_to, c_to), device_id_type=MESH
         )
 
     def owner_send(i, _):
@@ -276,25 +278,7 @@
             total = part if total is None else total + part
         out_ref[e] = total
 
-    for j in range(3):
-        for p in range(2):
-            for c_to in range(2):
-                here, _, far_copy = gather_parts(j, p, c_to)
-                pl.when(jnp.logical_not(here))(lambda: far_copy().wait_send())
-    for g in range(3):
-
-        def sent(i, _):
-            exchange(g, i).wait_send()
-            return 0
-
-        lax.fori_loop(1, 32, sent, 0)
-
-    def sent_small(i, _):
-        reduce_copy(i).wait_send()
-        owner_copy(i).wait_send()
-        return 0
-
-    lax.fori_loop(1, 16, sent_small, 0)
+    pltpu.make_async_copy(r2.at[pl.ds(0, 15)], r2.at[pl.ds(0, 15)], s_send).wait()
 
 
 def solution(mesh):
@@ -315,9 +299,9 @@
                 vm((3, 4, 2, NG, NG), bf),
                 vm((512, 256), bf),
                 vm((512, 256), bf),
-                vm((2, 1024, 128), f32),
-                vm((3, 32, 4, 16, 128), bf),
-                vm((3, 4, 512, 128), bf),
+                vm((1024, 128), f32),
+                vm((6, 32, 2, 16, 128), bf),
+                vm((6, 2, 512, 128), bf),
                 vm((4, 128, 128), f32),
                 vm((4, 4, 32, 128), bf),
                 vm((16, 32, 128), bf),
@@ -325,13 +309,13 @@
                 vm((16, 8, 128), f32),
                 vm((16, 8, 128), f32),
                 pltpu.SemaphoreType.DMA((7,)),
-                pltpu.SemaphoreType.DMA((12,)),
-                pltpu.SemaphoreType.DMA((3, 4)),
-                pltpu.SemaphoreType.DMA((3, 32)),
-                pltpu.SemaphoreType.DMA((3,)),
-                pltpu.SemaphoreType.DMA((16,)),
+                pltpu.SemaphoreType.DMA((6, 4)),
+                pltpu.SemaphoreType.DMA((6, 4)),
+                pltpu.SemaphoreType.DMA((6,)),
+                pltpu.SemaphoreType.DMA((6,)),
                 pltpu.SemaphoreType.DMA,
-                pltpu.SemaphoreType.DMA((16,)),
+                pltpu.SemaphoreType.DMA,
+                pltpu.SemaphoreType.DMA,
                 pltpu.SemaphoreType.DMA,
             ],
             compiler_params=pltpu.CompilerParams(collective_id=0, has_side_effects=True),

time: 64 us -> 60.9 us (0.952)
  Pallas kernels: 62.3 us -> 59.2 us
    pallas_call x1, Pallas kernels: 62.3 us -> 59.2 us  [local(): pl.pallas_call(kernel, out_shape=jax.ShapeDtypeStruct((2, NG, 32), f32),...]
where the time goes in v2:
time: 60.9 us; the launch traced here: 60.8 us
  Pallas kernels  59.2 us (97%)
  local copies, waits for them, and re-layouts  1.59 us (3%)
    pallas_call x1, Pallas kernels, local(): pl.pallas_call(kernel, out_shape=jax.ShapeDtypeStruct((2, NG, 32), f32),...  59.2 us
    pallas_call x1, local copies, waits for them, and re-layouts, local(): pl.pallas_call(kernel, out_shape=jax.ShapeDtypeStruct((2, NG, 32), f32),...  1.59 us

profile of v2, /device:TPU:1, one launch (start us, length us, event | category | flops | bytes accessed | tf_op | source)
XLA Modules:
  0.0 60.8 jit_solution(1648737427212227931)
XLA Ops:
  0.0 59.2 %shard_map.73 = f32[2,128,32]{2,1,0:T(8,128)} custom-call(f32[4,2,128,128]{3,2,1,0:T(8,128)} %x_hbm.1, bf16[256,256]{1,0:T(8,128)(2,1)} %constant.12.clone.t1_hbm, bf16[256,256]{1,0:T(8,128)(2,1)} %constant.13.clone.t2_hbm, bf16[512,512]{1,0:T(8,128)(2,1)} %constant.14.clone.t3_hbm, bf16[128,128]{1,0:T(8,128)(2,1)} %constant.15.clone.mir_hbm, ...), custom_call_target="tpu_custom_call" | custom-call | tf_op jit(solution)/shard_map/pallas_call | solution.py:289
  59.2 1.6 %copy.8 = f32[2,128,32]{1,2,0:T(8,128)} copy(f32[2,128,32]{2,1,0:T(8,128)} %shard_map.73) | data formatting | bytes 65536 | tf_op jit(solution)/shard_map/pallas_call | solution.py:289

commit v3 on v2

--- a/solution.py
+++ b/solution.py
@@ -15,6 +15,9 @@
 BF16 = ml_dtypes.bfloat16
 PIECES = ((0, 0), (1, 0), (1, 1), (0, 1), (2, 0), (2, 1))
 UNITS = ((3, 0, 0, 1, 1.0), (4, 0, 1, 1, 1.0), (5, 2, 0, 1, 1.0), (5, 2, 0, 0, 2.0), (6, 2, 1, 1, 1.0), (6, 2, 1, 0, 2.0))
+
+
+AHEAD = 3
 
 
 def ky_order():
@@ -142,12 +145,15 @@
 
         return here, local_copy, far_copy
 
-    for n in range(6):
+    def start_piece(n):
         for p in range(2):
             for c_to in range(2):
                 here, local_copy, far_copy = gather_parts(n, p, c_to)
                 pl.when(here)(lambda: local_copy().start())
                 pl.when(jnp.logical_not(here))(lambda: far_copy().start())
+
+    for n in range(AHEAD):
+        start_piece(n)
 
     def wait_piece(n):
         j, o = PIECES[n]
@@ -168,6 +174,8 @@
     for g, (needs, jl, ol, jr, _) in enumerate(UNITS):
         while held < needs:
             wait_piece(held)
+            if held + AHEAD < 6:
+                start_piece(held + AHEAD)
             held += 1
         for k in range(4):
             left = orb[jl, k, ol]

time: 60.9 us -> 59 us (0.969)
  Pallas kernels: 59.2 us -> 57 us
    pallas_call x1, Pallas kernels: 59.2 us -> 57 us  [local(): pl.pallas_call(kernel, out_shape=jax.ShapeDtypeStruct((2, NG, 32), f32),...]
where the time goes in v3:
time: 59 us; the launch traced here: 58.6 us
  Pallas kernels  57 us (97%)
  local copies, waits for them, and re-layouts  1.59 us (3%)
    pallas_call x1, Pallas kernels, local(): pl.pallas_call(kernel, out_shape=jax.ShapeDtypeStruct((2, NG, 32), f32),...  57 us
    pallas_call x1, local copies, waits for them, and re-layouts, local(): pl.pallas_call(kernel, out_shape=jax.ShapeDtypeStruct((2, NG, 32), f32),...  1.59 us

profile of v3, /device:TPU:1, one launch (start us, length us, event | category | flops | bytes accessed | tf_op | source)
XLA Modules:
  0.0 58.6 jit_solution(8872287274813554452)
XLA Ops:
  0.0 57.0 %shard_map.73 = f32[2,128,32]{2,1,0:T(8,128)} custom-call(f32[4,2,128,128]{3,2,1,0:T(8,128)} %x_hbm.1, bf16[256,256]{1,0:T(8,128)(2,1)} %constant.12.clone.t1_hbm, bf16[256,256]{1,0:T(8,128)(2,1)} %constant.13.clone.t2_hbm, bf16[512,512]{1,0:T(8,128)(2,1)} %constant.14.clone.t3_hbm, bf16[128,128]{1,0:T(8,128)(2,1)} %constant.15.clone.mir_hbm, ...), custom_call_target="tpu_custom_call" | custom-call | tf_op jit(solution)/shard_map/pallas_call | solution.py:297
  57.0 1.6 %copy.8 = f32[2,128,32]{1,2,0:T(8,128)} copy(f32[2,128,32]{2,1,0:T(8,128)} %shard_map.73) | data formatting | bytes 65536 | tf_op jit(solution)/shard_map/pallas_call | solution.py:297

commit v4 on v3

--- a/solution.py
+++ b/solution.py
@@ -189,18 +189,19 @@
             grid_rows[pl.ds(k * NG, NG), :] = second[:NG]
             grid_rows[pl.ds((4 + k) * NG, NG), :] = second[NG:]
 
-        def turn(d, _):
+        def turn(i):
+            yx_to, c_to = plane_peer(i)
+            d = yx_to * 2 + c_to
             for pair in range(2):
                 both_ky = [grid_rows[pl.ds(d * 4 + pair * 2 + i, 8, stride=NG), :] for i in range(2)]
                 msg[g, d, pair] = jnp.concatenate(both_ky, axis=0).astype(jnp.bfloat16)
-            return 0
-
-        lax.fori_loop(0, 32, turn, 0, unroll=4)
 
         def send(i, _):
+            turn(lax.rem(i + 1, 32))
             exchange(g, i).start()
             return 0
 
+        turn(1)
         lax.fori_loop(1, 32, send, 0)
         pltpu.make_async_copy(
             msg.at[g, d_me], got.at[g, :, pl.ds(pl.multiple_of(d_me * 16, 16), 16)], a_recv.at[g]

time: 59 us -> 58.7 us (level)
  no operation moved by 1% of the time
where the time goes in v4:
time: 58.7 us; the launch traced here: 58.2 us
  Pallas kernels  56.6 us (96%)
  local copies, waits for them, and re-layouts  1.59 us (3%)
    pallas_call x1, Pallas kernels, local(): pl.pallas_call(kernel, out_shape=jax.ShapeDtypeStruct((2, NG, 32), f32),...  56.6 us
    pallas_call x1, local copies, waits for them, and re-layouts, local(): pl.pallas_call(kernel, out_shape=jax.ShapeDtypeStruct((2, NG, 32), f32),...  1.59 us

profile of v4, /device:TPU:1, one launch (start us, length us, event | category | flops | bytes accessed | tf_op | source)
XLA Modules:
  0.0 58.2 jit_solution(15166200971597854654)
XLA Ops:
  0.0 56.6 %shard_map.73 = f32[2,128,32]{2,1,0:T(8,128)} custom-call(f32[4,2,128,128]{3,2,1,0:T(8,128)} %x_hbm.1, bf16[256,256]{1,0:T(8,128)(2,1)} %constant.12.clone.t1_hbm, bf16[256,256]{1,0:T(8,128)(2,1)} %constant.13.clone.t2_hbm, bf16[512,512]{1,0:T(8,128)(2,1)} %constant.14.clone.t3_hbm, bf16[128,128]{1,0:T(8,128)(2,1)} %constant.15.clone.mir_hbm, ...), custom_call_target="tpu_custom_call" | custom-call | tf_op jit(solution)/shard_map/pallas_call | solution.py:298
  56.6 1.6 %copy.8 = f32[2,128,32]{1,2,0:T(8,128)} copy(f32[2,128,32]{2,1,0:T(8,128)} %shard_map.73) | data formatting | bytes 65536 | tf_op jit(solution)/shard_map/pallas_call | solution.py:298
